TPU v7x, 32 devices: a whole 2x2x4 slice. The times are simulated.
32 devices in a mesh: lat: 8 (over z, y), tok: 4 (over x, core).
Axes of the slice: x: 2, y: 2, z: 4, core: 2. Of those that a mesh axis runs over, the one named last changes fastest.
Arguments:
- coefficients: bfloat16 [256, 16, 128], P(('lat', 'tok')), may hold values from 0 to 2
- block_ids: int32 [256, 16], P(('lat', 'tok')), may hold values from 0 to 1023, all different within a row; in each aligned block of 32 rows (0 to 31, 32 to 63, ...) at most 2 rows name the same one
- counts: int32 [256], P(('lat', 'tok')), may hold values from 10 to 16
- decoder: bfloat16 [1, 131072, 5120], P(None, 'lat', 'tok'), may hold values from -0.125 to 0.125
- bias: float32 [1, 5120], P(None, 'tok'), may hold values from -3 to 3
Outputs:
- recon: bfloat16 [1, 256, 5120], P(None, 'lat', 'tok')
Inputs may be any that keep to these rules, and one draw needn't show every extreme that they name: `block_ids`: the 16 slots of a token name different blocks. Among the tokens of one index of lat (aligned blocks of 32 rows), no block is named by more than 2 slots, live or padding, and some block is named by exactly 2. `counts`: slots below a token's count are live, the others padding.
All inputs are finite; a program needn't handle non-finite values.
Results may differ from a plain program's by a relative error of at most 0.001.
Values may be sent and summed in bfloat16 or wider, within the bound.
A program may use at most 128 MiB of HBM per device.

v0:
```python
import jax
import jax.numpy as jnp
from jax import lax
from jax.sharding import PartitionSpec as P


def shards(coefficients, block_ids, counts, decoder, bias):
    lat_count = lax.axis_size("lat")
    gathered_coeffs, gathered_ids, gathered_counts = (
        lax.all_gather(coefficients, "tok", axis=0, tiled=True),
        lax.all_gather(block_ids, "tok", axis=0, tiled=True),
        lax.all_gather(counts, "tok", axis=0, tiled=True),
    )
    tok_rows, slot_count = gathered_ids.shape
    block_size = gathered_coeffs.shape[2]
    layers, lat_latents, width_part = decoder.shape
    blocks_dev = lat_latents // block_size
    blocks_total = blocks_dev * lat_count
    capacity = max(2, tok_rows * slot_count * 2 // blocks_total)
    is_live = lax.broadcasted_iota(jnp.int32, (tok_rows, slot_count), 1) < gathered_counts[:, None]
    live_coeffs = jnp.where(
        is_live[:, :, None], gathered_coeffs, jnp.zeros((), gathered_coeffs.dtype)
    )
    flat_ids = gathered_ids.reshape(-1)
    serial = jnp.arange(flat_ids.shape[0], dtype=jnp.int32)
    matches = (flat_ids[:, None] == flat_ids[None, :]) & (serial[None, :] < serial[:, None])
    ranked = jnp.sum(matches.astype(jnp.int32), axis=1)
    position = flat_ids * capacity + ranked
    outgoing = jnp.zeros((blocks_total * capacity, block_size), gathered_coeffs.dtype)
    outgoing = outgoing.at[position].set(live_coeffs.reshape(-1, block_size))
    outgoing = outgoing.reshape(lat_count, blocks_dev * capacity, block_size)
    local_blocks = decoder.reshape(layers, blocks_dev, block_size, width_part)
    token_of = (
        jnp.full((blocks_total * capacity,), -1, jnp.int32).at[position].set(serial // slot_count)
    )
    token_of = token_of.reshape(lat_count, blocks_dev * capacity)
    incoming, tokens_in = (
        lax.all_to_all(outgoing, "lat", split_axis=0, concat_axis=0, tiled=True),
        lax.all_to_all(token_of, "lat", split_axis=0, concat_axis=0, tiled=True),
    )
    incoming = incoming.reshape(lat_count, blocks_dev, capacity, block_size)
    partial_rows = jnp.einsum(
        "sbmk,lbkd->sbmld", incoming, local_blocks, preferred_element_type=jnp.float32
    )
    partial_rows = partial_rows.reshape(-1, layers, width_part)
    source_base = lax.broadcasted_iota(jnp.int32, tokens_in.shape, 0) * tok_rows
    global_row = jnp.where(tokens_in >= 0, source_base + tokens_in, -1).reshape(-1)
    row_count = tok_rows * lax.axis_size("lat")
    target = global_row - jnp.int32(0)
    in_range = (global_row >= 0) & (target >= 0) & (target < row_count)
    target = jnp.where(in_range, target, row_count)
    empty_rows = jnp.zeros((row_count, layers, width_part), jnp.float32)
    summed_rows = lax.psum_scatter(
        empty_rows.at[target].add(partial_rows, mode="drop"), "lat", scatter_dimension=0, tiled=True
    )
    summed = jnp.transpose(summed_rows, (1, 0, 2))
    return (summed + bias[:, None, :]).astype(jnp.bfloat16)


def solution(mesh):
    in_specs = (
        P(("lat", "tok"), None, None),
        P(("lat", "tok"), None),
        P(("lat", "tok")),
        P(None, "lat", "tok"),
        P(None, "tok"),
    )
    out_specs = P(None, "lat", "tok")
    return jax.shard_map(shards, mesh=mesh, in_specs=in_specs, out_specs=out_specs, check_vma=False)
```

profile of v0, /device:TPU:0, one launch (start us, length us, event | category | flops | bytes accessed | tf_op | source)
XLA Modules:
  0.0 201.6 jit_solution(16010455425182599753)
XLA Ops:
  6.5 6.4 %all_gather.9 = s32[32,16]{1,0:T(8,128)S(1)} all-gather(s32[8,16]{1,0:T(8,128)} %param.6), channel_id=1, replica_groups=mesh['lat'=8,'tok'=4] {'tok'}, dimensions={0}, use_global_device_ids=true | all-gather | bytes 2560 | tf_op jit(solution)/shard_map/all_gather | solution.py:11
  12.9 0.1 eq.15
  13.0 0.1 mul.25
  13.1 0.3 convert_reduce_fusion
  13.3 3.0 %scatter_custom_fusion = s32[2048]{0:T(1024)} fusion(s32[512]{0:T(512)S(1)} %bitcast.42, s32[512]{0:T(512)S(1)} %add_select_fusion, s32[]{:T(128)} %constant.12.clone.1), kind=kCustom, calls=%fused_computation.24 | custom fusion | bytes 8196 | tf_op jit(solution)/shard_map/scatter | solution.py:34
  16.4 6.3 %all-to-all-start = ((s32[8,1,256]{2,1,0:T(1,128)}), s32[8,1,256]{2,1,0:T(1,128)S(1)}, u32[]{:S(2)}, u32[]{:S(2)}) async-start(s32[8,1,256]{2,1,0:T(1,128)} %bitcast.2), calls=%async_computation | async-start | bytes 16384 | tf_op jit(solution)/shard_map/all_to_all | solution.py:39
  22.6 5.6 %all_gather.11 = bf16[32,16,128]{2,1,0:T(8,128)(2,1)S(1)} all-gather(bf16[8,16,128]{2,1,0:T(8,128)(2,1)} %param.5), channel_id=1, replica_groups=mesh['lat'=8,'tok'=4] {'tok'}, dimensions={0}, use_global_device_ids=true | all-gather | bytes 163840 | tf_op jit(solution)/shard_map/all_gather | solution.py:10
  28.2 1.3 dynamic-slice
  30.3 0.9 dynamic-update-slice
  31.1 4.9 %all-reduce = s32[32]{0:T(128)S(1)} all-reduce(s32[32]{0:T(128)S(1)} %dynamic-update-slice), channel_id=1, replica_groups=mesh['lat'=8,'tok'=4] {'tok'}, use_global_device_ids=true, to_apply=%add | all-reduce | flops 32 | bytes 256
  36.0 0.1 iota_compare_fusion.1
  36.1 0.1 broadcast_select_fusion
  36.2 2.6 %scatter_custom_fusion.1 = bf16[2048,128]{1,0:T(8,128)(2,1)} fusion(s32[512]{0:T(512)S(1)} %bitcast.43, bf16[512,128]{1,0:T(8,128)(2,1)S(1)} %bitcast.37, bf16[]{:T(256)} %constant.37.clone.1), kind=kCustom, calls=%fused_computation.9 | custom fusion | bytes 524290 | tf_op jit(solution)/shard_map/scatter | solution.py:30
  38.8 0.0 all-to-all-done
  38.8 6.0 %all-to-all-start.1 = ((bf16[8,256,128]{2,1,0:T(8,128)(2,1)}), bf16[8,256,128]{2,1,0:T(8,128)(2,1)S(1)}, u32[]{:S(2)}, u32[]{:S(2)}) async-start(bf16[8,256,128]{2,1,0:T(8,128)(2,1)} %bitcast.7), calls=%async_computation.1 | async-start | bytes 1048576 | tf_op jit(solution)/shard_map/all_to_all | solution.py:38
  44.8 0.2 reduce-scatter.2.cloned.1.call-start
  45.1 0.1 broadcast_bitcast_fusion
  45.2 13.8 %all-to-all-done.1 = bf16[8,256,128]{2,1,0:T(8,128)(2,1)S(1)} async-done(((bf16[8,256,128]{2,1,0:T(8,128)(2,1)}), bf16[8,256,128]{2,1,0:T(8,128)(2,1)S(1)}, u32[]{:S(2)}, u32[]{:S(2)}) %all-to-all-start.1) | async-done | bytes 524320 | tf_op jit(solution)/shard_map/all_to_all | solution.py:38
  59.0 0.3 copy.10
  59.3 19.9 %convolution_bitcast_fusion = f32[8,128,2,1,1280]{4,0,2,1,3:T(8,128)} fusion(bf16[8,128,2,128]{3,0,2,1:T(8,128)(2,1)S(1)} %bitcast.36, bf16[128,128,1280,1]{2,1,3,0:T(8,128)(2,1)} %bitcast.34), kind=kOutput, calls=%fused_computation.3 | convolution fusion | flops 671088640 | bytes 52953088 | tf_op jit(solution)/shard_map/sbmk,lbkd->sbmld/dot_general | solution.py:42
  79.2 16.0 %copy.11 = f32[8,128,2,1,1280]{4,2,1,0,3:T(2,128)} copy(f32[8,128,2,1,1280]{4,0,2,1,3:T(8,128)} %convolution_bitcast_fusion) | data formatting | bytes 20971520 | tf_op jit(solution)/shard_map/sbmk,lbkd->sbmld/transpose | solution.py:42
  95.3 0.0 copy-start
  95.3 13.3 %reshape.198 = f32[2048,1280]{1,0:T(8,128)} reshape(f32[8,128,2,1,1280]{4,2,1,0,3:T(2,128)} %copy.11) | data formatting | bytes 20971520 | tf_op jit(solution)/shard_map/reshape | solution.py:45
  108.6 21.3 %scatter_custom_fusion.2 = f32[256,1280]{1,0:T(8,128)} fusion(s32[2048]{0:T(1024)S(1)} %bitcast.40, f32[2048,1280]{1,0:T(8,128)} %reshape.198, f32[]{:T(128)} %constant.11.clone.1), kind=kCustom, calls=%fused_computation.7 | custom fusion | flops 2621440 | bytes 1311232 | tf_op jit(solution)/shard_map/scatter-add | solution.py:54
  129.9 0.0 reduce-scatter.2.cloned.1.call-update
  129.9 0.0 copy-done
  130.0 63.3 %reduce-scatter.2.cloned.1.call-done = f32[32,1,1280]{2,0,1:T(8,128)} async-done(((f32[256,1,1280]{2,0,1:T(8,128)}), f32[32,1,1280]{2,0,1:T(8,128)}) %reduce-scatter.2.cloned.1.call-update) | async-done | bytes 163856 | tf_op jit(solution)/shard_map/reduce_scatter | solution.py:53
  193.2 1.6 fusion.5
  (8 shorter events, 0.1 us)
Async XLA Ops:
  16.4 22.5 %all-to-all-start = ((s32[8,1,256]{2,1,0:T(1,128)}), s32[8,1,256]{2,1,0:T(1,128)S(1)}, u32[]{:S(2)}, u32[]{:S(2)}) async-start(s32[8,1,256]{2,1,0:T(1,128)} %bitcast.2), calls=%async_computation | async-start | bytes 16384 | tf_op jit(solution)/shard_map/all_to_all | solution.py:39
  38.8 20.2 %all-to-all-start.1 = ((bf16[8,256,128]{2,1,0:T(8,128)(2,1)}), bf16[8,256,128]{2,1,0:T(8,128)(2,1)S(1)}, u32[]{:S(2)}, u32[]{:S(2)}) async-start(bf16[8,256,128]{2,1,0:T(8,128)(2,1)} %bitcast.7), calls=%async_computation.1 | async-start | bytes 1048576 | tf_op jit(solution)/shard_map/all_to_all | solution.py:38
  44.8 148.4 %reduce-scatter.2.cloned.1.call-start = ((), (), s32[]{:S(2)}) async-start(), calls=%async_computation.3 | async-start | bytes 1474560 | tf_op jit(solution)/shard_map/reduce_scatter | solution.py:53
  95.3 34.6 %copy-start = (f32[1,1280]{1,0:T(1,128)S(1)}, f32[1,1280]{1,0:T(1,128)}, u32[]{:S(2)}) copy-start(f32[1,1280]{1,0:T(1,128)} %param.9) | copy-start | bytes 15364
Sparse Core Ops, SparseCore 0:
  130.0 63.1 reduce-scatter.1
where the time goes:
time: 202 us
  waiting for transfers between devices  77.1 us (38%)
  local copies, waits for them, and re-layouts  37.7 us (19%)
  other arithmetic  23.4 us (12%)
  matrix products  19.9 us (10%)
  blocking collectives  16.9 us (8%)
  between operations  14.2 us (7%)
  starting transfers between devices  12.5 us (6%)
    reduce_scatter x1, waiting for transfers between devices, shards(): lax.psum_scatter(empty_rows.at[target].add(partial_rows, mode='drop'), 'l...  63.3 us
    scatter-add x1, other arithmetic, shards(): empty_rows.at[target].add(partial_rows, mode='drop')  21.3 us
    dot_general x1, matrix products, shards(): jnp.einsum('sbmk,lbkd->sbmld', incoming, local_blocks, preferred_element_...  19.9 us
    transpose x1, local copies, waits for them, and re-layouts, shards(): jnp.einsum('sbmk,lbkd->sbmld', incoming, local_blocks, preferred_element_...  16 us
    all_to_all x1, waiting for transfers between devices, shards(): lax.all_to_all(outgoing, 'lat', split_axis=0, concat_axis=0, tiled=True)  13.8 us
    reshape x1, local copies, waits for them, and re-layouts, shards(): partial_rows = partial_rows.reshape(-1, layers, width_part)  13.3 us
    all_gather x1, blocking collectives, shards(): lax.all_gather(block_ids, 'tok', axis=0, tiled=True)  6.36 us
    all_to_all x1, starting transfers between devices, shards(): lax.all_to_all(token_of, 'lat', split_axis=0, concat_axis=0, tiled=True)  6.27 us
  transfers between devices with their start and end apart: 3, of which 2 were waited for; matrix products, arithmetic and copies ran while one was open for 3% of the time, Pallas kernels for 0%

commit v1 on v0

v1 whole, which is shorter than its diff:
```python
import functools

import jax
import jax.numpy as jnp
from jax import lax
from jax.experimental import pallas as pl
from jax.experimental.pallas import tpu as pltpu
from jax.sharding import PartitionSpec as P

MESH = pl.DeviceIdType.MESH
F32 = jnp.float32
BF16 = jnp.bfloat16


def largest_divisor(total, limit, unit):
    best = unit
    for size in range(unit, limit + 1, unit):
        if total % size == 0:
            best = size
    return best


def kernel(cfg, counts_ref, ids_ref, bias_ref, coeff_ref, dec_ref, out_ref,
           gath, wv, amat, part, yrecv, ysum, zrecv,
           own_sem, w_sem, zs, zr, hs, hr, cs, cr, ys, yr, ps, pr):
    nl, nt, tpd, slots, block, nb, chunks, wc, kstep, mstep, bstep = cfg
    nz, nx = nl // 2, nt // 2
    rows_dev = tpd * slots
    pack_rows = gath.shape[4]
    half = rows_dev // 2
    lat, tok = lax.axis_index("lat"), lax.axis_index("tok")
    z, y = lat // 2, lat % 2
    x, core = tok // 2, tok % 2
    oy, oc = 1 - y, 1 - core
    latents = nb * block

    w_copies = []
    for c in range(chunks):
        cols = pl.ds(c * wc, wc)
        cp = pltpu.make_async_copy(dec_ref.at[:, cols], wv.at[:, cols], w_sem.at[c])
        w_copies.append(cp)
    own = pltpu.make_async_copy(coeff_ref, gath.at[z, y, x, core, pl.ds(0, rows_dev)], own_sem)
    own.start()
    for cp in w_copies:
        cp.start()

    ids = ids_ref[...]
    trow = lax.broadcasted_iota(jnp.int32, (tpd, slots), 0)
    scol = lax.broadcasted_iota(jnp.int32, (tpd, slots), 1)
    live_to = jnp.zeros((tpd, slots), jnp.int32)
    for t in range(tpd):
        live_to = jnp.where(trow == t, counts_ref[t], live_to)
    idf = ids.astype(F32)
    owner = jnp.floor((idf + 0.5) * (1.0 / nb))
    within = idf - owner * nb
    owner = jnp.where(scol < live_to, owner, -1.0)
    srow = lax.broadcasted_iota(jnp.int32, (slots, rows_dev), 0)
    jcol = lax.broadcasted_iota(jnp.int32, (slots, rows_dev), 1)
    spread = jnp.where(jcol % slots == srow, 1.0, 0.0).astype(F32)
    t8 = lax.broadcasted_iota(jnp.int32, (tpd, rows_dev), 0)
    j8 = lax.broadcasted_iota(jnp.int32, (tpd, rows_dev), 1)
    mine = (j8 >= t8 * slots) & (j8 < (t8 + 1) * slots)

    def as_row(v):
        wide = jnp.dot(v, spread, preferred_element_type=F32)
        return jnp.sum(jnp.where(mine, wide, 0.0), axis=0, keepdims=True)

    r16 = lax.broadcasted_iota(jnp.int32, (pack_rows - rows_dev, rows_dev), 0)
    packed = jnp.where(r16 == 0, as_row(owner), jnp.where(r16 == 1, as_row(within), 0.0))
    gath[z, y, x, core, rows_dev:pack_rows, :] = packed.astype(BF16)

    zpeer = [lax.rem(z + d, nz) for d in range(1, nz)]
    xpeer = [lax.rem(x + d, nx) for d in range(1, nx)]
    peers = [(p * 2 + y, tok) for p in zpeer]
    peers += [(z * 2 + oy, tok), (lat, x * 2 + oc)]
    peers += [(lat, p * 2 + core) for p in xpeer]
    barrier = pltpu.get_barrier_semaphore()
    for p in peers:
        pl.semaphore_signal(barrier, inc=1, device_id=p, device_id_type=MESH)
    pl.semaphore_wait(barrier, len(peers))

    sent = []

    def send(src, dst, ssem, rsem, dev):
        cp = pltpu.make_async_remote_copy(src_ref=src, dst_ref=dst, send_sem=ssem,
                                          recv_sem=rsem, device_id=dev, device_id_type=MESH)
        cp.start()
        sent.append(cp)
        return cp

    def move(view, ssem, rsem, dev):
        return send(view, view, ssem, rsem, dev)

    h0, h1 = pl.ds(0, half), pl.ds(half, pack_rows - half)
    yp, cp_dev = (z * 2 + oy, tok), (lat, x * 2 + oc)
    own.wait()
    first = [move(gath.at[z, y, x, core], zs.at[d], zr.at[d], (zpeer[d] * 2 + y, tok))
             for d in range(nz - 1)]
    for cp in first:
        cp.wait_recv()
    xa = [move(gath.at[:, y, x, core, h0], hs.at[0, d], hr.at[0, d], (lat, xpeer[d] * 2 + core))
          for d in range(nx - 1)]
    ya = move(gath.at[:, y, x, core, h1], hs.at[1, 0], hr.at[1, 0], yp)
    got = [move(gath.at[:, y, x, core], cs.at[0], cr.at[0], cp_dev)]
    for cp in xa:
        cp.wait_recv()
    yb = move(gath.at[:, y, :, core, h0], hs.at[2, 0], hr.at[2, 0], yp)
    ya.wait_recv()
    xb = [move(gath.at[:, :, x, core, h1], hs.at[3, d], hr.at[3, d], (lat, xpeer[d] * 2 + core))
          for d in range(nx - 1)]
    for d in range(nx - 1):
        src = lax.rem(x + nx - 1 - d, nx)
        got.append(move(gath.at[:, y, src, core, h0], cs.at[1 + d], cr.at[1 + d], cp_dev))
    base = nx
    got.append(move(gath.at[:, oy, x, core, h1], cs.at[base], cr.at[base], cp_dev))

    lat_f = lat.astype(F32)
    pair = 2 * rows_dev
    pt = 2 * tpd
    tb = lax.broadcasted_iota(jnp.int32, (pt, pair), 0)
    jb = lax.broadcasted_iota(jnp.int32, (pt, pair), 1)
    diag = jnp.where((jb >= tb * slots) & (jb < (tb + 1) * slots), 1.0, 0.0).astype(BF16)

    def build(zz, yy, xx):
        locs = []
        for c in range(2):
            tags = gath[zz, yy, xx, c, rows_dev:pack_rows, :].astype(F32)
            locs.append(jnp.where(tags[0:1] == lat_f, tags[1:2], -1.0))
        loc = jnp.concatenate(locs, axis=1)
        loc = jnp.broadcast_to(loc, (pt, pair)).astype(BF16)
        rhs = gath[zz, yy, xx, :, 0:rows_dev, :].reshape(pair, block)
        row0 = pl.multiple_of(((zz * 2 + yy) * nx + xx) * pt, pt)
        for b0 in range(0, nb, bstep):
            hot = jnp.concatenate(
                [jnp.where(loc == jnp.asarray(b, BF16), diag, jnp.zeros((), BF16))
                 for b in range(b0, b0 + bstep)], axis=0)
            rows = jnp.dot(hot, rhs, preferred_element_type=F32).astype(BF16)
            for i in range(bstep):
                amat[pl.ds(row0, pt), (b0 + i) * block:(b0 + i + 1) * block] = (
                    rows[i * pt:(i + 1) * pt])

    got[0].wait_recv()

    @pl.loop(0, nz)
    def _(zz):
        build(zz, y, x)

    yb.wait_recv()
    got.append(move(gath.at[:, oy, :, core, h0], cs.at[base + 1], cr.at[base + 1], cp_dev))
    for d in range(nx - 1):
        xb[d].wait_recv()
        src = lax.rem(x + nx - 1 - d, nx)
        got.append(move(gath.at[:, :, src, core, h1], cs.at[base + 2 + d], cr.at[base + 2 + d], cp_dev))
    for cp in got[1:]:
        cp.wait_recv()

    @pl.loop(0, nz * (2 * nx - 1))
    def _(i):
        zz, q = i // (2 * nx - 1), i % (2 * nx - 1) + 1
        build(zz, lax.rem(y + q // nx, 2), lax.rem(x + q % nx, nx))

    tokens = amat.shape[0]
    per_lat = tokens // nl

    def matmul(c):
        cols = pl.ds(c * wc, wc)

        @pl.loop(0, tokens // mstep)
        def _(m):
            rows = pl.ds(pl.multiple_of(m * mstep, mstep), mstep)
            lats = pl.ds(m * (mstep // (2 * per_lat)), mstep // (2 * per_lat))
            shape = (mstep // (2 * per_lat), 2, per_lat, wc)

            def term(k):
                kk = pl.ds(pl.multiple_of(k * kstep, kstep), kstep)
                return jnp.dot(amat[rows, kk], wv[kk, cols],
                               preferred_element_type=F32).reshape(shape)

            part[c, lats] = term(0)

            @pl.loop(1, latents // kstep)
            def _(k):
                part[c, lats] += term(k)

    def y_start(c):
        return send(part.at[c, :, oy], yrecv.at[c], ys.at[c], yr.at[c], yp)

    def z_start(c, ycp):
        ycp.wait_recv()
        ysum[c] = part[c, :, y] + yrecv[c]
        return [send(ysum.at[c, zpeer[d]], zrecv.at[c, d], ps.at[c, d], pr.at[c, d],
                     (zpeer[d] * 2 + y, tok)) for d in range(nz - 1)]

    def finish(c, zcps):
        total = ysum[c, z] + bias_ref[:, c * wc:(c + 1) * wc]
        for d, cp in enumerate(zcps):
            cp.wait_recv()
            total += zrecv[c, d]
        out_ref[:, c * wc:(c + 1) * wc] = total.astype(out_ref.dtype)

    ycps, zcps = {}, {}
    for c in range(chunks + 2):
        if c < chunks:
            w_copies[c].wait()
            matmul(c)
            ycps[c] = y_start(c)
        if 0 <= c - 1 < chunks:
            zcps[c - 1] = z_start(c - 1, ycps[c - 1])
        if 0 <= c - 2 < chunks:
            finish(c - 2, zcps[c - 2])
    for cp in sent:
        cp.wait_send()


def shards(coefficients, block_ids, counts, decoder, bias):
    nl, nt = lax.axis_size("lat"), lax.axis_size("tok")
    tpd, slots, block = coefficients.shape
    layers, latents, width = decoder.shape
    nb = latents // block
    tokens = tpd * nl * nt
    nz, nx = nl // 2, nt // 2
    per_lat = tokens // nl
    rows_dev = tpd * slots
    pack_rows = rows_dev + 16
    wc = largest_divisor(width, 256, 128)
    chunks = width // wc
    kstep = largest_divisor(latents, 2048, block)
    mstep = largest_divisor(tokens, 256, 2 * per_lat)
    bstep = largest_divisor(nb, 32, 1)
    cfg = (nl, nt, tpd, slots, block, nb, chunks, wc, kstep, mstep, bstep)
    dma = pltpu.SemaphoreType.DMA
    vmem = pl.BlockSpec(memory_space=pltpu.VMEM)
    hbm = pl.BlockSpec(memory_space=pl.ANY)
    flops = 2 * tokens * latents * width
    outs = []
    for layer in range(layers):
        outs.append(pl.pallas_call(
            functools.partial(kernel, cfg),
            out_shape=jax.ShapeDtypeStruct((per_lat, width), BF16),
            in_specs=[pl.BlockSpec(memory_space=pltpu.SMEM), vmem, vmem, hbm, hbm],
            out_specs=vmem,
            scratch_shapes=[
                pltpu.VMEM((nz, 2, nx, 2, pack_rows, block), BF16),
                pltpu.VMEM((latents, width), BF16),
                pltpu.VMEM((tokens, latents), BF16),
                pltpu.VMEM((chunks, nz, 2, per_lat, wc), F32),
                pltpu.VMEM((chunks, nz, per_lat, wc), F32),
                pltpu.VMEM((chunks, nz, per_lat, wc), F32),
                pltpu.VMEM((chunks, nz - 1, per_lat, wc), F32),
                dma, dma((chunks,)),
                dma((nz - 1,)), dma((nz - 1,)),
                dma((4, nx - 1)), dma((4, nx - 1)),
                dma((2 * nx + 1,)), dma((2 * nx + 1,)),
                dma((chunks,)), dma((chunks,)),
                dma((chunks, nz - 1)), dma((chunks, nz - 1)),
            ],
            compiler_params=pltpu.CompilerParams(
                collective_id=layer, has_side_effects=True, vmem_limit_bytes=66000000),
            cost_estimate=pl.CostEstimate(
                flops=flops, bytes_accessed=latents * width * 2, transcendentals=0),
        )(counts, block_ids, bias[layer:layer + 1], coefficients.reshape(rows_dev, block),
          decoder[layer]))
    return jnp.stack(outs)


def solution(mesh):
    in_specs = (
        P(("lat", "tok"), None, None),
        P(("lat", "tok"), None),
        P(("lat", "tok")),
        P(None, "lat", "tok"),
        P(None, "tok"),
    )
    out_specs = P(None, "lat", "tok")
    return jax.shard_map(shards, mesh=mesh, in_specs=in_specs, out_specs=out_specs, check_vma=False)
```

time: 202 us -> 64.1 us (0.32)
  waiting for transfers between devices: 77.1 us -> 0 us
  Pallas kernels: 0 us -> 62.4 us
  local copies, waits for them, and re-layouts: 37.7 us -> 1.53 us
  other arithmetic: 23.4 us -> 0 us
  matrix products: 19.9 us -> 0 us
  blocking collectives: 16.9 us -> 0 us
  between operations: 14.2 us -> 0.01 us
  starting transfers between devices: 12.5 us -> 0 us
    reduce_scatter x1 -> x0, waiting for transfers between devices: 63.3 us -> none  [shards(): lax.psum_scatter(empty_rows.at[target].add(partial_rows, mode='drop'), 'l...]
    pallas_call x0 -> x1, Pallas kernels: none -> 62.4 us  [shards(): pl.pallas_call(functools.partial(kernel, cfg), out_shape=jax.ShapeDtypeSt...]
    scatter-add x1 -> x0, other arithmetic: 21.3 us -> none  [shards(): empty_rows.at[target].add(partial_rows, mode='drop')]
    dot_general x1 -> x0, matrix products: 19.9 us -> none  [shards(): jnp.einsum('sbmk,lbkd->sbmld', incoming, local_blocks, preferred_element_...]
    transpose x1 -> x0, local copies, waits for them, and re-layouts: 16 us -> none  [shards(): jnp.einsum('sbmk,lbkd->sbmld', incoming, local_blocks, preferred_element_...]
    all_to_all x2 -> x0, waiting for transfers between devices: 13.8 us -> none  [the longest x1 13.8 us: shards(): lax.all_to_all(outgoing, 'lat', split_axis=0, concat_axis=0, tiled=True)]
    reshape x1 -> x0, local copies, waits for them, and re-layouts: 13.3 us -> none  [shards(): partial_rows = partial_rows.reshape(-1, layers, width_part)]
    all_to_all x2 -> x0, starting transfers between devices: 12.3 us -> none  [the longest x1 6.27 us: shards(): lax.all_to_all(token_of, 'lat', split_axis=0, concat_axis=0, tiled=True)]
  transfers between devices with their start and end apart: 3 -> 0, of which waited for: 2 -> 0; matrix products, arithmetic and copies ran while one was open for 3% -> 0% of each run, Pallas kernels for 0% -> 0%
where the time goes in v1:
time: 64.1 us; the launch traced here: 63.9 us
  Pallas kernels  62.4 us (97%)
  local copies, waits for them, and re-layouts  1.53 us (2%)
    pallas_call x1, Pallas kernels, shards(): pl.pallas_call(functools.partial(kernel, cfg), out_shape=jax.ShapeDtypeSt...  62.4 us
    unnamed x1, local copies, waits for them, and re-layouts  1.53 us

profile of v1, /device:TPU:0, one launch (start us, length us, event | category | flops | bytes accessed | tf_op | source)
XLA Modules:
  0.0 63.9 jit_solution(2109322066232909622)
XLA Ops:
  0.0 62.4 %shard_map.55 = bf16[32,1280]{1,0:T(8,128)(2,1)} custom-call(s32[8]{0:T(128)} %counts_ref.1, s32[8,16]{1,0:T(8,128)} %ids_ref.1, f32[1,1280]{1,0:T(1,128)} %bias_ref.1, bf16[128,128]{1,0:T(8,128)(2,1)} %bitcast.5, bf16[16384,1280]{1,0:T(8,128)(2,1)} %bitcast.3), custom_call_target="tpu_custom_call" | custom-call | flops 10737418240 | bytes 41943040 | tf_op jit(solution)/shard_map/pallas_call | solution.py:237
  62.4 1.5 %copy.7 = bf16[1,32,1280]{2,1,0:T(8,128)(2,1)} copy(bf16[1,32,1280]{2,1,0:T(8,128)(2,1)} %bitcast.4) | data formatting | bytes 163840

commit v2 on v1

--- a/solution.py
+++ b/solution.py
@@ -20,29 +20,47 @@
     return best
 
 
+def flip(z, k):
+    step, out = 1, z
+    while step <= k:
+        if k & step:
+            out = out + step - 2 * step * ((z // step) % 2)
+        step *= 2
+    return out
+
+
 def kernel(cfg, counts_ref, ids_ref, bias_ref, coeff_ref, dec_ref, out_ref,
            gath, wv, amat, part, yrecv, ysum, zrecv,
-           own_sem, w_sem, zs, zr, hs, hr, cs, cr, ys, yr, ps, pr):
-    nl, nt, tpd, slots, block, nb, chunks, wc, kstep, mstep, bstep = cfg
+           own_sem, w_sem, zs, zr, xs, xr, vs, vr, ds, dr, cs, cr, ys, yr, ps, pr):
+    nl, nt, tpd, slots, block, nb, widths, rw, kstep, mstep, bstep, wsplit = cfg
     nz, nx = nl // 2, nt // 2
     rows_dev = tpd * slots
     pack_rows = gath.shape[4]
-    half = rows_dev // 2
     lat, tok = lax.axis_index("lat"), lax.axis_index("tok")
     z, y = lat // 2, lat % 2
     x, core = tok // 2, tok % 2
     oy, oc = 1 - y, 1 - core
     latents = nb * block
+    offs = [sum(widths[:i]) for i in range(len(widths))]
 
     w_copies = []
-    for c in range(chunks):
-        cols = pl.ds(c * wc, wc)
-        cp = pltpu.make_async_copy(dec_ref.at[:, cols], wv.at[:, cols], w_sem.at[c])
-        w_copies.append(cp)
+    for off, w in zip(offs, widths):
+        parts = wsplit * w // widths[0]
+        for r in range(parts):
+            at = (pl.ds(r * (latents // parts), latents // parts), pl.ds(off, w))
+            w_copies.append(pltpu.make_async_copy(dec_ref.at[at], wv.at[at],
+                                                  w_sem.at[len(w_copies)]))
+    w_first = [sum(wsplit * w // widths[0] for w in widths[:i]) for i in range(len(widths) + 1)]
+    issued = [0]
+
+    def stream(upto):
+        while issued[0] < min(upto, len(w_copies)):
+            w_copies[issued[0]].start()
+            issued[0] += 1
+
     own = pltpu.make_async_copy(coeff_ref, gath.at[z, y, x, core, pl.ds(0, rows_dev)], own_sem)
     own.start()
-    for cp in w_copies:
-        cp.start()
+    stream(2)
 
     ids = ids_ref[...]
     trow = lax.broadcasted_iota(jnp.int32, (tpd, slots), 0)
@@ -69,7 +87,12 @@
     packed = jnp.where(r16 == 0, as_row(owner), jnp.where(r16 == 1, as_row(within), 0.0))
     gath[z, y, x, core, rows_dev:pack_rows, :] = packed.astype(BF16)
 
-    zpeer = [lax.rem(z + d, nz) for d in range(1, nz)]
+    if nz & (nz - 1):
+        zto = [lax.rem(z + k, nz) for k in range(nz)]
+        zof = [lax.rem(z + nz - k, nz) for k in range(nz)]
+    else:
+        zto = zof = [flip(z, k) for k in range(nz)]
+    zpeer = zto[1:]
     xpeer = [lax.rem(x + d, nx) for d in range(1, nx)]
     peers = [(p * 2 + y, tok) for p in zpeer]
     peers += [(z * 2 + oy, tok), (lat, x * 2 + oc)]
@@ -90,29 +113,6 @@
 
     def move(view, ssem, rsem, dev):
         return send(view, view, ssem, rsem, dev)
-
-    h0, h1 = pl.ds(0, half), pl.ds(half, pack_rows - half)
-    yp, cp_dev = (z * 2 + oy, tok), (lat, x * 2 + oc)
-    own.wait()
-    first = [move(gath.at[z, y, x, core], zs.at[d], zr.at[d], (zpeer[d] * 2 + y, tok))
-             for d in range(nz - 1)]
-    for cp in first:
-        cp.wait_recv()
-    xa = [move(gath.at[:, y, x, core, h0], hs.at[0, d], hr.at[0, d], (lat, xpeer[d] * 2 + core))
-          for d in range(nx - 1)]
-    ya = move(gath.at[:, y, x, core, h1], hs.at[1, 0], hr.at[1, 0], yp)
-    got = [move(gath.at[:, y, x, core], cs.at[0], cr.at[0], cp_dev)]
-    for cp in xa:
-        cp.wait_recv()
-    yb = move(gath.at[:, y, :, core, h0], hs.at[2, 0], hr.at[2, 0], yp)
-    ya.wait_recv()
-    xb = [move(gath.at[:, :, x, core, h1], hs.at[3, d], hr.at[3, d], (lat, xpeer[d] * 2 + core))
-          for d in range(nx - 1)]
-    for d in range(nx - 1):
-        src = lax.rem(x + nx - 1 - d, nx)
-        got.append(move(gath.at[:, y, src, core, h0], cs.at[1 + d], cr.at[1 + d], cp_dev))
-    base = nx
-    got.append(move(gath.at[:, oy, x, core, h1], cs.at[base], cr.at[base], cp_dev))
 
     lat_f = lat.astype(F32)
     pair = 2 * rows_dev
@@ -139,75 +139,121 @@
                 amat[pl.ds(row0, pt), (b0 + i) * block:(b0 + i + 1) * block] = (
                     rows[i * pt:(i + 1) * pt])
 
-    got[0].wait_recv()
-
-    @pl.loop(0, nz)
-    def _(zz):
-        build(zz, y, x)
-
-    yb.wait_recv()
-    got.append(move(gath.at[:, oy, :, core, h0], cs.at[base + 1], cr.at[base + 1], cp_dev))
-    for d in range(nx - 1):
-        xb[d].wait_recv()
-        src = lax.rem(x + nx - 1 - d, nx)
-        got.append(move(gath.at[:, :, src, core, h1], cs.at[base + 2 + d], cr.at[base + 2 + d], cp_dev))
-    for cp in got[1:]:
-        cp.wait_recv()
-
-    @pl.loop(0, nz * (2 * nx - 1))
-    def _(i):
-        zz, q = i // (2 * nx - 1), i % (2 * nx - 1) + 1
-        build(zz, lax.rem(y + q // nx, 2), lax.rem(x + q % nx, nx))
+    yp, cp_dev = (z * 2 + oy, tok), (lat, x * 2 + oc)
+    xof = [lax.rem(x + nx - 1 - e, nx) for e in range(nx - 1)]
+    own.wait()
+    zc = [None] + [move(gath.at[z, y, x, core], zs.at[k], zr.at[k], (zto[k] * 2 + y, tok))
+                   for k in range(1, nz)]
+    xc, vc, dc, cc = {}, {}, {}, {}
+
+    def to_core(k, q, yy, xx):
+        v = gath.at[zof[k], yy, xx, core]
+        cc[k, q] = move(v, cs.at[k, q], cr.at[k, q], cp_dev)
+
+    for step in range(nz + 3):
+        k = step
+        if k < nz:
+            if k:
+                pltpu.make_async_remote_copy(
+                    src_ref=gath.at[zof[k], y, x, core], dst_ref=gath.at[zof[k], y, x, core],
+                    send_sem=zs.at[k], recv_sem=zr.at[k], device_id=(zto[k] * 2 + y, tok),
+                    device_id_type=MESH).wait_recv()
+            v = gath.at[zof[k], y, x, core]
+            for e in range(nx - 1):
+                xc[k, e] = move(v, xs.at[k, e], xr.at[k, e], (lat, xpeer[e] * 2 + core))
+            vc[k] = move(v, vs.at[k], vr.at[k], yp)
+            to_core(k, 0, y, x)
+        stream(4 + 3 * (step + 1))
+        k = step - 1
+        if 0 <= k < nz:
+            for e in range(nx - 1):
+                xc[k, e].wait_recv()
+                if k % 2 == 0:
+                    dc[k, e] = move(gath.at[zof[k], y, xof[e], core], ds.at[k, e], dr.at[k, e], yp)
+                to_core(k, 2 + e, y, xof[e])
+            vc[k].wait_recv()
+            if k % 2:
+                for e in range(nx - 1):
+                    dc[k, e] = move(gath.at[zof[k], oy, x, core], ds.at[k, e], dr.at[k, e],
+                                    (lat, xpeer[e] * 2 + core))
+            to_core(k, 1, oy, x)
+        k = step - 2
+        if 0 <= k < nz:
+            for e in range(nx - 1):
+                dc[k, e].wait_recv()
+                to_core(k, nx + 1 + e, oy, xof[e])
+            cc[k, 0].wait_recv()
+            build(zof[k], y, x)
+            cc[k, 1].wait_recv()
+            build(zof[k], oy, x)
+            for e in range(nx - 1):
+                cc[k, 2 + e].wait_recv()
+                build(zof[k], y, xof[e])
+        k = step - 3
+        if 0 <= k < nz:
+            for e in range(nx - 1):
+                cc[k, nx + 1 + e].wait_recv()
+                build(zof[k], oy, xof[e])
+    stream(len(w_copies))
 
     tokens = amat.shape[0]
     per_lat = tokens // nl
 
-    def matmul(c):
-        cols = pl.ds(c * wc, wc)
+    def matmul(i):
+        cols = pl.ds(offs[i], widths[i])
 
         @pl.loop(0, tokens // mstep)
         def _(m):
             rows = pl.ds(pl.multiple_of(m * mstep, mstep), mstep)
             lats = pl.ds(m * (mstep // (2 * per_lat)), mstep // (2 * per_lat))
-            shape = (mstep // (2 * per_lat), 2, per_lat, wc)
+            shape = (mstep // (2 * per_lat), 2, per_lat, widths[i])
 
             def term(k):
                 kk = pl.ds(pl.multiple_of(k * kstep, kstep), kstep)
                 return jnp.dot(amat[rows, kk], wv[kk, cols],
                                preferred_element_type=F32).reshape(shape)
 
-            part[c, lats] = term(0)
+            part[lats, :, :, cols] = term(0)
 
             @pl.loop(1, latents // kstep)
             def _(k):
-                part[c, lats] += term(k)
+                part[lats, :, :, cols] += term(k)
 
     def y_start(c):
-        return send(part.at[c, :, oy], yrecv.at[c], ys.at[c], yr.at[c], yp)
+        cols = pl.ds(c * rw, rw)
+        return send(part.at[:, oy, :, cols], yrecv.at[:, :, cols], ys.at[c], yr.at[c], yp)
 
     def z_start(c, ycp):
+        cols = pl.ds(c * rw, rw)
         ycp.wait_recv()
-        ysum[c] = part[c, :, y] + yrecv[c]
-        return [send(ysum.at[c, zpeer[d]], zrecv.at[c, d], ps.at[c, d], pr.at[c, d],
-                     (zpeer[d] * 2 + y, tok)) for d in range(nz - 1)]
+        ysum[:, :, cols] = part[:, y, :, cols] + yrecv[:, :, cols]
+        return [send(ysum.at[zto[k], :, cols], zrecv.at[k - 1, :, cols], ps.at[c, k - 1],
+                     pr.at[c, k - 1], (zto[k] * 2 + y, tok)) for k in range(1, nz)]
 
     def finish(c, zcps):
-        total = ysum[c, z] + bias_ref[:, c * wc:(c + 1) * wc]
+        cols = pl.ds(c * rw, rw)
+        total = ysum[z, :, cols] + bias_ref[:, cols]
         for d, cp in enumerate(zcps):
             cp.wait_recv()
-            total += zrecv[c, d]
-        out_ref[:, c * wc:(c + 1) * wc] = total.astype(out_ref.dtype)
+            total += zrecv[d, :, cols]
+        out_ref[:, cols] = total.astype(out_ref.dtype)
 
     ycps, zcps = {}, {}
-    for c in range(chunks + 2):
-        if c < chunks:
-            w_copies[c].wait()
-            matmul(c)
+    pend = []
+    for i in range(len(widths)):
+        for cp in w_copies[w_first[i]:w_first[i + 1]]:
+            cp.wait()
+        matmul(i)
+        now = list(range(offs[i] // rw, (offs[i] + widths[i]) // rw))
+        for c in now:
             ycps[c] = y_start(c)
-        if 0 <= c - 1 < chunks:
-            zcps[c - 1] = z_start(c - 1, ycps[c - 1])
-        if 0 <= c - 2 < chunks:
-            finish(c - 2, zcps[c - 2])
+        for c in pend:
+            zcps[c] = z_start(c, ycps[c])
+        pend = now
+    for c in pend:
+        zcps[c] = z_start(c, ycps[c])
+    for c in zcps:
+        finish(c, zcps[c])
     for cp in sent:
         cp.wait_send()
 
@@ -222,12 +268,18 @@
     per_lat = tokens // nl
     rows_dev = tpd * slots
     pack_rows = rows_dev + 16
-    wc = largest_divisor(width, 256, 128)
-    chunks = width // wc
-    kstep = largest_divisor(latents, 2048, block)
+    unit = largest_divisor(width, 256, 128)
+    widths = [unit]
+    while sum(widths) < width:
+        widths.append(min(2 * unit, width - sum(widths)))
+    rw = 128
+    chunks = width // rw
+    wsplit = 4
+    pieces = sum(wsplit * w // unit for w in widths)
+    kstep = largest_divisor(latents, 4096, block)
     mstep = largest_divisor(tokens, 256, 2 * per_lat)
     bstep = largest_divisor(nb, 32, 1)
-    cfg = (nl, nt, tpd, slots, block, nb, chunks, wc, kstep, mstep, bstep)
+    cfg = (nl, nt, tpd, slots, block, nb, tuple(widths), rw, kstep, mstep, bstep, wsplit)
     dma = pltpu.SemaphoreType.DMA
     vmem = pl.BlockSpec(memory_space=pltpu.VMEM)
     hbm = pl.BlockSpec(memory_space=pl.ANY)
@@ -243,14 +295,16 @@
                 pltpu.VMEM((nz, 2, nx, 2, pack_rows, block), BF16),
                 pltpu.VMEM((latents, width), BF16),
                 pltpu.VMEM((tokens, latents), BF16),
-                pltpu.VMEM((chunks, nz, 2, per_lat, wc), F32),
-                pltpu.VMEM((chunks, nz, per_lat, wc), F32),
-                pltpu.VMEM((chunks, nz, per_lat, wc), F32),
-                pltpu.VMEM((chunks, nz - 1, per_lat, wc), F32),
-                dma, dma((chunks,)),
-                dma((nz - 1,)), dma((nz - 1,)),
-                dma((4, nx - 1)), dma((4, nx - 1)),
-                dma((2 * nx + 1,)), dma((2 * nx + 1,)),
+                pltpu.VMEM((nz, 2, per_lat, width), F32),
+                pltpu.VMEM((nz, per_lat, width), F32),
+                pltpu.VMEM((nz, per_lat, width), F32),
+                pltpu.VMEM((nz - 1, per_lat, width), F32),
+                dma, dma((pieces,)),
+                dma((nz,)), dma((nz,)),
+                dma((nz, nx - 1)), dma((nz, nx - 1)),
+                dma((nz,)), dma((nz,)),
+                dma((nz, nx - 1)), dma((nz, nx - 1)),
+                dma((nz, 2 * nx)), dma((nz, 2 * nx)),
                 dma((chunks,)), dma((chunks,)),
                 dma((chunks, nz - 1)), dma((chunks, nz - 1)),
             ],

time: 64.1 us -> 52.7 us (0.82)
  Pallas kernels: 62.4 us -> 50.9 us
    pallas_call x1, Pallas kernels: 62.4 us -> 50.9 us  [shards(): pl.pallas_call(functools.partial(kernel, cfg), out_shape=jax.ShapeDtypeSt...]
where the time goes in v2:
time: 52.7 us; the launch traced here: 52.5 us
  Pallas kernels  50.9 us (97%)
  local copies, waits for them, and re-layouts  1.53 us (3%)
    pallas_call x1, Pallas kernels, shards(): pl.pallas_call(functools.partial(kernel, cfg), out_shape=jax.ShapeDtypeSt...  50.9 us
    unnamed x1, local copies, waits for them, and re-layouts  1.53 us

profile of v2, /device:TPU:0, one launch (start us, length us, event | category | flops | bytes accessed | tf_op | source)
XLA Modules:
  0.0 52.5 jit_solution(10682928429852433847)
XLA Ops:
  0.0 50.9 %shard_map.55 = bf16[32,1280]{1,0:T(8,128)(2,1)} custom-call(s32[8]{0:T(128)} %counts_ref.1, s32[8,16]{1,0:T(8,128)} %ids_ref.1, f32[1,1280]{1,0:T(1,128)} %bias_ref.1, bf16[128,128]{1,0:T(8,128)(2,1)} %bitcast.5, bf16[16384,1280]{1,0:T(8,128)(2,1)} %bitcast.3), custom_call_target="tpu_custom_call" | custom-call | flops 10737418240 | bytes 41943040 | tf_op jit(solution)/shard_map/pallas_call | solution.py:289
  50.9 1.5 %copy.7 = bf16[1,32,1280]{2,1,0:T(8,128)(2,1)} copy(bf16[1,32,1280]{2,1,0:T(8,128)(2,1)} %bitcast.4) | data formatting | bytes 163840

commit v3 on v2

--- a/solution.py
+++ b/solution.py
@@ -199,25 +199,26 @@
     tokens = amat.shape[0]
     per_lat = tokens // nl
 
-    def matmul(i):
+    def matmul(i, between):
         cols = pl.ds(offs[i], widths[i])
-
-        @pl.loop(0, tokens // mstep)
-        def _(m):
-            rows = pl.ds(pl.multiple_of(m * mstep, mstep), mstep)
-            lats = pl.ds(m * (mstep // (2 * per_lat)), mstep // (2 * per_lat))
-            shape = (mstep // (2 * per_lat), 2, per_lat, widths[i])
-
-            def term(k):
-                kk = pl.ds(pl.multiple_of(k * kstep, kstep), kstep)
-                return jnp.dot(amat[rows, kk], wv[kk, cols],
+        ksteps = latents // kstep
+        for k in range(ksteps):
+            kk = pl.ds(k * kstep, kstep)
+
+            @pl.loop(0, tokens // mstep)
+            def _(m):
+                rows = pl.ds(pl.multiple_of(m * mstep, mstep), mstep)
+                lats = pl.ds(m * (mstep // (2 * per_lat)), mstep // (2 * per_lat))
+                shape = (mstep // (2 * per_lat), 2, per_lat, widths[i])
+                term = jnp.dot(amat[rows, kk], wv[kk, cols],
                                preferred_element_type=F32).reshape(shape)
-
-            part[lats, :, :, cols] = term(0)
-
-            @pl.loop(1, latents // kstep)
-            def _(k):
-                part[lats, :, :, cols] += term(k)
+                if k == 0:
+                    part[lats, :, :, cols] = term
+                else:
+                    part[lats, :, :, cols] += term
+
+            if k == ksteps * 3 // 4 - 1:
+                between()
 
     def y_start(c):
         cols = pl.ds(c * rw, rw)
@@ -243,12 +244,18 @@
     for i in range(len(widths)):
         for cp in w_copies[w_first[i]:w_first[i + 1]]:
             cp.wait()
-        matmul(i)
+
+        def early():
+            if pend:
+                zcps[pend[0]] = z_start(pend[0], ycps[pend[0]])
+
+        matmul(i, early)
         now = list(range(offs[i] // rw, (offs[i] + widths[i]) // rw))
         for c in now:
             ycps[c] = y_start(c)
         for c in pend:
-            zcps[c] = z_start(c, ycps[c])
+            if c not in zcps:
+                zcps[c] = z_start(c, ycps[c])
         pend = now
     for c in pend:
         zcps[c] = z_start(c, ycps[c])
@@ -268,15 +275,15 @@
     per_lat = tokens // nl
     rows_dev = tpd * slots
     pack_rows = rows_dev + 16
-    unit = largest_divisor(width, 256, 128)
+    unit = largest_divisor(width, 640, 128)
     widths = [unit]
     while sum(widths) < width:
-        widths.append(min(2 * unit, width - sum(widths)))
+        widths.append(unit)
     rw = 128
     chunks = width // rw
-    wsplit = 4
+    wsplit = 8
     pieces = sum(wsplit * w // unit for w in widths)
-    kstep = largest_divisor(latents, 4096, block)
+    kstep = largest_divisor(latents, 2048, block)
     mstep = largest_divisor(tokens, 256, 2 * per_lat)
     bstep = largest_divisor(nb, 32, 1)
     cfg = (nl, nt, tpd, slots, block, nb, tuple(widths), rw, kstep, mstep, bstep, wsplit)

time: 52.7 us -> 54 us (1.025)
  Pallas kernels: 50.9 us -> 52.2 us
    pallas_call x1, Pallas kernels: 50.9 us -> 52.2 us  [shards(): pl.pallas_call(functools.partial(kernel, cfg), out_shape=jax.ShapeDtypeSt...]
where the time goes in v3:
time: 54 us; the launch traced here: 53.8 us
  Pallas kernels  52.2 us (97%)
  local copies, waits for them, and re-layouts  1.53 us (3%)
    pallas_call x1, Pallas kernels, shards(): pl.pallas_call(functools.partial(kernel, cfg), out_shape=jax.ShapeDtypeSt...  52.2 us
    unnamed x1, local copies, waits for them, and re-layouts  1.53 us

profile of v3, /device:TPU:0, one launch (start us, length us, event | category | flops | bytes accessed | tf_op | source)
XLA Modules:
  0.0 53.8 jit_solution(4065046563334391081)
XLA Ops:
  0.0 52.2 %shard_map.55 = bf16[32,1280]{1,0:T(8,128)(2,1)} custom-call(s32[8]{0:T(128)} %counts_ref.1, s32[8,16]{1,0:T(8,128)} %ids_ref.1, f32[1,1280]{1,0:T(1,128)} %bias_ref.1, bf16[128,128]{1,0:T(8,128)(2,1)} %bitcast.5, bf16[16384,1280]{1,0:T(8,128)(2,1)} %bitcast.3), custom_call_target="tpu_custom_call" | custom-call | flops 10737418240 | bytes 41943040 | tf_op jit(solution)/shard_map/pallas_call | solution.py:296
  52.2 1.5 %copy.7 = bf16[1,32,1280]{2,1,0:T(8,128)(2,1)} copy(bf16[1,32,1280]{2,1,0:T(8,128)(2,1)} %bitcast.4) | data formatting | bytes 163840
